TPU v7x, 32 devices: a whole 2x2x4 slice. The times are simulated.
32 devices in a mesh: grp: 2 (over x), scan: 16 (over z, y, core).
Axes of the slice: x: 2, y: 2, z: 4, core: 2. Of those that a mesh axis runs over, the one named last changes fastest.
Arguments:
- patterns: bfloat16 [3072, 64, 256], P(('grp', 'scan')), parts along dimension 0, may hold values from -6 to 6
- templates: bfloat16 [32, 64, 256], P('scan'), may hold values from -6 to 6
- radius_bin: int32 [64], replicated, may hold values from 0 to 7
- radial_gain: float32 [8], replicated, may hold values from 0.25 to 4
- orientation: int32 [32, 1], replicated, may hold values from 0 to 15
Outputs:
- corr_map: float32 [3072, 32], P(('grp', 'scan')), parts along dimension 0
- orient_map: float32 [3072, 16], P(('grp', 'scan')), parts along dimension 0
There are 2 independent parts, one for each index of `grp`. A program takes and returns all parts, laid end to end along the dimension named above; an argument that names none is the same for every part. Nothing has to cross between parts.
Inputs may be any that keep to these rules, and one draw needn't show every extreme that they name: Every orientation group holds at least one template.
All inputs are finite; a program needn't handle non-finite values.
Results may differ from a plain program's by a relative error of at most 0.0024.
Values may be sent and summed in bfloat16 or wider, within the bound.
No kernel may reach another device: no remote copies, remote signals or barrier semaphores. Data moves between devices by JAX's collectives and lax.ppermute only.
A program may use at most 128 MiB of HBM per device.

v0:
```python
import math
import jax
import jax.numpy as jnp
from jax import lax
from jax.sharding import PartitionSpec as P

RADII = 64
ANGLES = 256
GAINS = 8
TMPL_PER_GROUP = 2


def with_halo(shard, sides, width):
    for axis, dim in sides:
        size, length = (lax.axis_size(axis), shard.shape[dim])
        up = [(i, (i + 1) % size) for i in range(size - 1)]
        down = [(j, i) for i, j in up]
        last = lax.slice_in_dim(shard, length - width, length, axis=dim)
        leading = lax.slice_in_dim(shard, 0, width, axis=dim)
        before = lax.ppermute(last, axis, up)
        after = lax.ppermute(leading, axis, down)
        shard = jnp.concatenate([before, shard, after], axis=dim)
    return shard


def make_tables():
    half = ANGLES // 2
    along = jnp.arange(ANGLES, dtype=jnp.int32)
    modes = jnp.arange(half + 1, dtype=jnp.int32)
    phase = 2.0 * math.pi / ANGLES * (along[:, None] * modes[None, :] % ANGLES).astype(jnp.float32)
    basis = jnp.concatenate([jnp.cos(phase), jnp.sin(phase[:, 1:half])], axis=1).astype(
        jnp.bfloat16
    )
    factor_norm = 1.0 / (ANGLES * math.sqrt(RADII * ANGLES))
    mode_weight = jnp.where((modes == 0) | (modes == half), 1.0, 2.0).astype(jnp.float32)
    phase_rows = phase.T
    inverse = jnp.concatenate(
        [mode_weight[:, None] * jnp.cos(phase_rows), -mode_weight[:, None] * jnp.sin(phase_rows)],
        axis=0,
    )
    return (basis, (inverse * factor_norm).astype(jnp.bfloat16))


def spectrum(raw, basis):
    count = raw.shape[0]
    flat = raw.reshape(-1, ANGLES)
    spec = lax.dot_general(
        basis, flat, (((0,), (1,)), ((), ())), preferred_element_type=jnp.float32
    )
    return spec.reshape(ANGLES, count, RADII)


def mode_products(left, right):
    return jnp.einsum("kpr,ktr->ktp", left, right, preferred_element_type=jnp.float32)


def correlate(pat_spec, tmpl_spec, inverse):
    half = ANGLES // 2
    count = tmpl_spec.shape[1]
    pos_count = pat_spec.shape[1]
    pat_cos = pat_spec[: half + 1]
    pat_sin = pat_spec[half + 1 :]
    tmpl_cos = tmpl_spec[: half + 1]
    tmpl_sin = tmpl_spec[half + 1 :]
    both_cos = mode_products(pat_cos, tmpl_cos)
    both_sin = mode_products(pat_sin, tmpl_sin)
    cos_sin = mode_products(pat_cos[1:half], tmpl_sin)
    sin_cos = mode_products(pat_sin, tmpl_cos[1:half])
    edge = jnp.zeros((1, count, pos_count), jnp.float32)
    real_part = both_cos + jnp.concatenate([edge, both_sin, edge], axis=0)
    imag_part = jnp.concatenate([edge, cos_sin - sin_cos, edge], axis=0)
    cross = jnp.concatenate([real_part, imag_part], axis=0).astype(jnp.bfloat16)
    cross = cross.reshape(2 * (half + 1), count * pos_count)
    shifted = lax.dot_general(
        inverse, cross, (((0,), (0,)), ((), ())), preferred_element_type=jnp.float32
    )
    return jnp.max(shifted, axis=0).reshape(count, pos_count)


def block_of(count, limit):
    size = limit
    while size > 1:
        if count % size == 0:
            return size
        size = size // 2
    return 1


def correlate_into(carry, pat_spec, count, prepare, inverse):
    block_size = block_of(count, 64)

    def step(index, total):
        begin = index * block_size
        values = correlate(pat_spec, prepare(begin, block_size), inverse)
        return lax.dynamic_update_slice(total, values, (begin, jnp.int32(0)))

    return lax.fori_loop(0, count // block_size, step, carry)


def on_device(patterns, templates, radius_bin, radial_gain, orientation):
    basis, inverse = make_tables()
    pos_count = patterns.shape[0]
    total_tmpl = templates.shape[0] * lax.axis_size("scan")
    group_count = total_tmpl // TMPL_PER_GROUP
    onehot = (radius_bin[:, None] == jnp.arange(GAINS, dtype=jnp.int32)[None, :]).astype(
        jnp.float32
    )
    radius_weight = jnp.sum(onehot * radial_gain[None, :], axis=1)
    pat_spec = (spectrum(patterns, basis) * radius_weight[None, None, :]).astype(jnp.bfloat16)
    initial = jnp.zeros((total_tmpl, pos_count), jnp.float32)

    def raw_rows(piece):
        return lambda begin, size: spectrum(
            lax.dynamic_slice_in_dim(piece, begin, size, 0), basis
        ).astype(jnp.bfloat16)

    piece = lax.all_gather(templates, "scan", axis=0, tiled=True)
    by_template = correlate_into(initial, pat_spec, piece.shape[0], raw_rows(piece), inverse)
    corr_map = by_template.T
    groups = orientation[:, 0]
    member = groups[None, :] == jnp.arange(group_count, dtype=jnp.int32)[:, None]
    group_block = block_of(group_count, 16)
    member_blocks = member.reshape(group_count // group_block, group_block, total_tmpl)

    def group_max(mask):
        return jnp.max(jnp.where(mask[:, :, None], by_template[None, :, :], -jnp.inf), axis=1)

    best = lax.map(group_max, member_blocks).reshape(group_count, pos_count).T
    padded = with_halo(best, (("scan", 0),), 1)
    orient_map = 0.25 * (padded[:-2] + 2.0 * best + padded[2:])
    return (corr_map, orient_map)


def solution(mesh):
    placed = (P(("grp", "scan"), None, None), P("scan", None, None), P(), P(), P())
    return jax.shard_map(
        on_device,
        mesh=mesh,
        in_specs=placed,
        out_specs=(P(("grp", "scan"), None), P(("grp", "scan"), None)),
        check_vma=False,
    )
```

profile of v0, /device:TPU:5, one launch (start us, length us, event | category | flops | bytes accessed | tf_op | source)
XLA Modules:
  0.0 101.3 jit_solution(18244889343172042133)
XLA Ops:
  8.9 1.0 cosine_convert_fusion
  10.5 3.6 %multiply_convert_fusion = bf16[256,96,64]{0,1,2:T(8,128)(2,1)S(1)} fusion(f32[64]{0:T(128)S(1)} %select_reduce_fusion.1, bf16[96,64,256]{2,1,0:T(8,128)(2,1)S(1)} %copy-done, bf16[256,127]{1,0:T(8,128)(2,1)S(1)} %fusion.31, bf16[256,129]{1,0:T(8,128)(2,1)S(1)} %cosine_convert_fusion), kind=kOutput, calls=%fused_computation | convolution fusion | flops 808714240 | bytes 6422784 | tf_op jit(solution)/shard_map/dot_general | solution.py:47
  14.1 2.7 %fusion.41 = (bf16[127,96,64]{0,1,2:T(8,128)(2,1)}, bf16[127,96,64]{0,1,2:T(8,128)(2,1)}) fusion(bf16[256,96,64]{0,1,2:T(8,128)(2,1)S(1)} %multiply_convert_fusion), kind=kLoop, calls=%fused_computation.59 | loop fusion | bytes 6242304 | tf_op jit(solution)/shard_map/while/body/eval_jaxpr/slice | solution.py:62
  16.9 4.0 %copy.44 = bf16[127,96,64]{1,2,0:T(8,128)(2,1)} copy(bf16[127,96,64]{0,1,2:T(8,128)(2,1)} %get-tuple-element.28) | data formatting | bytes 3121152 | tf_op jit(solution)/shard_map/while/body/eval_jaxpr/slice | solution.py:67
  20.9 4.0 %copy.42 = bf16[127,96,64]{1,2,0:T(8,128)(2,1)} copy(bf16[127,96,64]{0,1,2:T(8,128)(2,1)} %get-tuple-element.20) | data formatting | bytes 3121152 | tf_op jit(solution)/shard_map/while/body/eval_jaxpr/slice | solution.py:62
  24.9 5.0 %copy.40 = bf16[129,96,64]{1,2,0:T(8,128)(2,1)} copy(bf16[129,96,64]{0,1,2:T(8,128)(2,1)} %bitcast.19) | data formatting | bytes 3170304 | tf_op jit(solution)/shard_map/while/body/eval_jaxpr/slice | solution.py:61
  29.9 1.2 %sine_multiply_fusion = (f32[129,256]{1,0:T(8,128)S(1)}, f32[129,256]{1,0:T(8,128)}) fusion(f32[129]{0:T(256)S(1)} %fusion.35, f32[129]{0:T(256)S(1)} %or_select_fusion), kind=kLoop, calls=%fused_computation.35 | loop fusion | flops 528384 | bytes 265224 | tf_op jit(solution)/shard_map/mul | solution.py:38
  31.1 17.7 %all-gather.2.cloned.1.call-done = bf16[32,64,256]{2,1,0:T(8,128)(2,1)} async-done(((bf16[2,64,256]{2,1,0:T(8,128)(2,1)}), bf16[32,64,256]{2,1,0:T(8,128)(2,1)}) %all-gather.2.cloned.1.call-update) | async-done | bytes 1048592 | tf_op jit(solution)/shard_map/all_gather | solution.py:117
  48.8 1.7 %convolution_convert_fusion = bf16[256,32,64]{0,2,1:T(8,128)(2,1)S(1)} fusion(bf16[32,64,256]{2,1,0:T(8,128)(2,1)} %all-gather.2.cloned.1.call-done, bf16[256,127]{1,0:T(8,128)(2,1)S(1)} %fusion.31, bf16[256,129]{1,0:T(8,128)(2,1)S(1)} %cosine_convert_fusion), kind=kOutput, calls=%fused_computation.14 | convolution fusion | flops 269221888 | bytes 2228224 | tf_op jit(solution)/shard_map/while/body/eval_jaxpr/dot_general | solution.py:47
  51.5 1.4 %fusion.42 = (bf16[127,32,64]{0,2,1:T(8,128)(2,1)}, bf16[127,32,64]{0,2,1:T(8,128)(2,1)}) fusion(bf16[256,32,64]{0,2,1:T(8,128)(2,1)S(1)} %convolution_convert_fusion), kind=kLoop, calls=%fused_computation.60 | loop fusion | bytes 2080768 | tf_op jit(solution)/shard_map/while/body/eval_jaxpr/slice | solution.py:68
  52.9 3.5 %copy.41 = bf16[127,32,64]{2,1,0:T(8,128)(2,1)} copy(bf16[127,32,64]{0,2,1:T(8,128)(2,1)} %get-tuple-element.30) | data formatting | bytes 1040384 | tf_op jit(solution)/shard_map/while/body/eval_jaxpr/slice | solution.py:64
  56.4 3.5 %copy.45 = bf16[127,32,64]{2,1,0:T(8,128)(2,1)} copy(bf16[127,32,64]{0,2,1:T(8,128)(2,1)} %get-tuple-element.29) | data formatting | bytes 1040384 | tf_op jit(solution)/shard_map/while/body/eval_jaxpr/slice | solution.py:68
  59.9 2.7 %fusion.45 = f32[127,32,96]{2,1,0:T(8,128)S(1)} fusion(bf16[127,32,64]{2,1,0:T(8,128)(2,1)} %copy.41, bf16[127,96,64]{1,2,0:T(8,128)(2,1)} %copy.44), kind=kOutput, calls=%fused_computation.63 | convolution fusion | flops 49938432 | bytes 3641344 | tf_op jit(solution)/shard_map/while/body/eval_jaxpr/kpr,ktr->ktp/dot_general | solution.py:54
  62.7 2.0 %fusion.44 = f32[127,32,96]{2,1,0:T(8,128)} fusion(bf16[127,32,64]{2,1,0:T(8,128)(2,1)S(1)} %copy-done.4, bf16[127,96,64]{1,2,0:T(8,128)(2,1)S(1)} %copy-done.1), kind=kOutput, calls=%fused_computation.62 | convolution fusion | flops 49938432 | bytes 3641344 | tf_op jit(solution)/shard_map/while/body/eval_jaxpr/kpr,ktr->ktp/dot_general | solution.py:54
  64.7 1.7 %subtract_convert_fusion = bf16[127,32,96]{2,1,0:T(8,128)(2,1)} fusion(f32[127,32,96]{2,1,0:T(8,128)S(1)} %fusion.45, bf16[127,32,64]{2,1,0:T(8,128)(2,1)S(1)} %copy-done.5, bf16[127,96,64]{1,2,0:T(8,128)(2,1)S(1)} %copy-done.1), kind=kOutput, calls=%fused_computation.5 | convolution fusion | flops 50718720 | bytes 4421632 | tf_op jit(solution)/shard_map/while/body/eval_jaxpr/kpr,ktr->ktp/dot_general | solution.py:54
  66.4 2.7 %copy.47 = bf16[127,32,96]{0,2,1:T(8,128)(2,1)} copy(bf16[127,32,96]{2,1,0:T(8,128)(2,1)} %subtract_convert_fusion) | data formatting | bytes 1560576 | tf_op jit(solution)/shard_map/convert.4
  69.1 2.4 %copy.48 = bf16[127,3072]{1,0:T(8,128)(2,1)} copy(bf16[127,3072]{0,1:T(8,128)(2,1)} %bitcast.21) | data formatting | bytes 1560576 | tf_op jit(solution)/shard_map/while/body/eval_jaxpr/concatenate | solution.py:72
  71.5 2.8 %copy.39 = bf16[129,32,64]{2,1,0:T(8,128)(2,1)} copy(bf16[129,32,64]{0,2,1:T(8,128)(2,1)} %bitcast.20) | data formatting | bytes 1056768 | tf_op jit(solution)/shard_map/while/body/eval_jaxpr/slice | solution.py:63
  74.3 4.3 %fusion.4 = bf16[129,32,96]{2,1,0:T(8,128)(2,1)} fusion(f32[1,32,96]{2,1,0:T(8,128)S(1)} %broadcast.63, f32[127,32,96]{2,1,0:T(8,128)} %fusion.44, bf16[129,32,64]{2,1,0:T(8,128)(2,1)} %copy.39, bf16[129,96,64]{1,2,0:T(8,128)(2,1)} %copy.40), kind=kOutput, calls=%fused_computation.4 | convolution fusion | flops 52310016 | bytes 4478976 | tf_op jit(solution)/shard_map/while/body/eval_jaxpr/kpr,ktr->ktp/dot_general | solution.py:54
  78.6 3.4 %concatenate.33 = bf16[129,3072]{1,0:T(8,128)(2,1)} reshape(bf16[129,32,96]{2,1,0:T(8,128)(2,1)} %fusion.4) | data formatting | bytes 1585152 | tf_op jit(solution)/shard_map/while/body/eval_jaxpr/concatenate | solution.py:72
  82.0 2.5 %fusion.13 = f32[3072]{0:T(1024)S(1)} fusion(bf16[1,3072]{1,0:T(2,128)(2,1)S(1)} %concatenate.34, bf16[127,3072]{1,0:T(8,128)(2,1)} %copy.48, bf16[129,3072]{1,0:T(8,128)(2,1)} %concatenate.33, f32[129,256]{1,0:T(8,128)S(1)} %get-tuple-element.37, f32[129,256]{1,0:T(8,128)S(1)} %copy-done.6), kind=kOutput, calls=%fused_computation.15 | convolution fusion | flops 413121024 | bytes 1855488 | tf_op jit(solution)/shard_map/while/body/eval_jaxpr/dot_general | solution.py:74
  84.7 3.2 %collective-permute-start = (f32[1,16]{0,1:T(8,128)S(1)}, f32[1,16]{0,1:T(8,128)S(1)}, u32[]{:S(2)}, u32[]{:S(2)}) collective-permute-start(f32[1,16]{0,1:T(8,128)S(1)} %get-tuple-element.31), channel_id=1, source_target_pairs={{0,1},{1,2},{2,3},{3,4},{4,5},{5,6},{6,7},{7,8},{8,9},{9,10},{10,1... | collective-permute-start | bytes 200 | tf_op jit(solution)/shard_map/ppermute | solution.py:20
  87.9 1.9 %collective-permute-start.1 = (f32[1,16]{0,1:T(8,128)S(1)}, f32[1,16]{0,1:T(8,128)S(1)}, u32[]{:S(2)}, u32[]{:S(2)}) collective-permute-start(f32[1,16]{0,1:T(8,128)S(1)} %get-tuple-element.36), channel_id=1, source_target_pairs={{1,0},{2,1},{3,2},{4,3},{5,4},{6,5},{7,6},{8,7},{9,8},{10,9},{11,1... | collective-permute-start | bytes 200 | tf_op jit(solution)/shard_map/ppermute | solution.py:21
  89.9 3.9 %collective-permute-done.1 = f32[1,16]{0,1:T(8,128)S(1)} collective-permute-done((f32[1,16]{0,1:T(8,128)S(1)}, f32[1,16]{0,1:T(8,128)S(1)}, u32[]{:S(2)}, u32[]{:S(2)}) %collective-permute-start.1) | collective-permute-done | bytes 96 | tf_op jit(solution)/shard_map/ppermute | solution.py:21
  (33 shorter events, 4.3 us)
Async XLA Ops:
  7.2 3.3 %copy-start = (bf16[96,64,256]{2,1,0:T(8,128)(2,1)S(1)}, bf16[96,64,256]{2,1,0:T(8,128)(2,1)}, u32[]{:S(2)}) copy-start(bf16[96,64,256]{2,1,0:T(8,128)(2,1)} %param.5) | copy-start | bytes 9437188
  7.2 41.6 %all-gather.2.cloned.1.call-start = ((), (), s32[]{:S(2)}) async-start(), calls=%async_computation | async-start | bytes 1114112 | tf_op jit(solution)/shard_map/all_gather | solution.py:117
  14.1 2.7 %copy-start.2 = (bf16[256,96,64]{0,1,2:T(8,128)(2,1)}, bf16[256,96,64]{0,1,2:T(8,128)(2,1)S(1)}, u32[]{:S(2)}) copy-start(bf16[256,96,64]{0,1,2:T(8,128)(2,1)S(1)} %multiply_convert_fusion) | copy-start | bytes 9437188
  24.9 5.0 %copy-start.8 = (s32[32,1]{0,1:T(1,128)S(1)}, s32[32,1]{0,1:T(1,128)}, u32[]{:S(2)}) copy-start(s32[32,1]{0,1:T(1,128)} %param.9) | copy-start | bytes 388
  50.6 1.0 copy-start.3
  59.9 2.7 %copy-start.1 = (bf16[127,96,64]{1,2,0:T(8,128)(2,1)S(1)}, bf16[127,96,64]{1,2,0:T(8,128)(2,1)}, u32[]{:S(2)}) copy-start(bf16[127,96,64]{1,2,0:T(8,128)(2,1)} %copy.42) | copy-start | bytes 4681732
  59.9 2.8 %copy-start.4 = (bf16[127,32,64]{2,1,0:T(8,128)(2,1)S(1)}, bf16[127,32,64]{2,1,0:T(8,128)(2,1)}, u32[]{:S(2)}) copy-start(bf16[127,32,64]{2,1,0:T(8,128)(2,1)} %copy.41) | copy-start | bytes 1560580
  62.7 2.0 %copy-start.5 = (bf16[127,32,64]{2,1,0:T(8,128)(2,1)S(1)}, bf16[127,32,64]{2,1,0:T(8,128)(2,1)}, u32[]{:S(2)}) copy-start(bf16[127,32,64]{2,1,0:T(8,128)(2,1)} %copy.45) | copy-start | bytes 1560580
  74.3 7.6 %copy-start.6 = (f32[129,256]{1,0:T(8,128)S(1)}, f32[129,256]{1,0:T(8,128)}, u32[]{:S(2)}) copy-start(f32[129,256]{1,0:T(8,128)} %get-tuple-element.38) | copy-start | bytes 396292
  84.5 10.0 %copy-start.7 = (f32[32,96]{1,0:T(8,128)}, f32[32,96]{1,0:T(8,128)S(1)}, u32[]{:S(2)}) copy-start(f32[32,96]{1,0:T(8,128)S(1)} %reshape.51) | copy-start | bytes 36868
  84.7 5.2 %collective-permute-start = (f32[1,16]{0,1:T(8,128)S(1)}, f32[1,16]{0,1:T(8,128)S(1)}, u32[]{:S(2)}, u32[]{:S(2)}) collective-permute-start(f32[1,16]{0,1:T(8,128)S(1)} %get-tuple-element.31), channel_id=1, source_target_pairs={{0,1},{1,2},{2,3},{3,4},{4,5},{5,6},{6,7},{7,8},{8,9},{9,10},{10,1... | collective-permute-start | bytes 200 | tf_op jit(solution)/shard_map/ppermute | solution.py:20
  87.9 5.9 %collective-permute-start.1 = (f32[1,16]{0,1:T(8,128)S(1)}, f32[1,16]{0,1:T(8,128)S(1)}, u32[]{:S(2)}, u32[]{:S(2)}) collective-permute-start(f32[1,16]{0,1:T(8,128)S(1)} %get-tuple-element.36), channel_id=1, source_target_pairs={{1,0},{2,1},{3,2},{4,3},{5,4},{6,5},{7,6},{8,7},{9,8},{10,9},{11,1... | collective-permute-start | bytes 200 | tf_op jit(solution)/shard_map/ppermute | solution.py:21
Sparse Core Ops, SparseCore 0:
  10.2 38.5 all-gather.1
where the time goes:
time: 102 us; the launch traced here: 101 us
  local copies, waits for them, and re-layouts  36.6 us (36%)
  waiting for transfers between devices  22.3 us (22%)
  matrix products  18.5 us (18%)
  between operations  14.2 us (14%)
  starting transfers between devices  5.19 us (5%)
  other arithmetic  4.61 us (5%)
    all_gather x1, waiting for transfers between devices, on_device(): piece = lax.all_gather(templates, 'scan', axis=0, tiled=True)  17.7 us
    dot_general x4, matrix products, mode_products(): jnp.einsum('kpr,ktr->ktp', left, right, preferred_element_type=jnp.float32)  10.6 us
    slice x2, local copies, waits for them, and re-layouts, correlate(): pat_sin = pat_spec[half + 1:]  6.72 us
    concatenate x3, local copies, waits for them, and re-layouts, correlate(): cross = jnp.concatenate([real_part, imag_part], axis=0).astype(jnp.bfloat16)  5.75 us
    dot_general x2, matrix products, spectrum(): lax.dot_general(basis, flat, (((0,), (1,)), ((), ())), preferred_element_...  5.37 us
    slice x1, local copies, waits for them, and re-layouts, correlate(): pat_cos = pat_spec[:half + 1]  4.96 us
    slice x2, local copies, waits for them, and re-layouts, correlate(): sin_cos = mode_products(pat_sin, tmpl_cos[1:half])  4.9 us
    slice x1, local copies, waits for them, and re-layouts, correlate(): cos_sin = mode_products(pat_cos[1:half], tmpl_sin)  4 us
  transfers between devices with their start and end apart: 3, of which 2 were waited for; matrix products, arithmetic and copies ran while one was open for 23% of the time, Pallas kernels for 0%

commit v1 on v0

--- a/solution.py
+++ b/solution.py
@@ -8,6 +8,23 @@
 ANGLES = 256
 GAINS = 8
 TMPL_PER_GROUP = 2
+
+
+def joined_along(blocks, dim):
+    blocks = jnp.moveaxis(blocks, 0, dim)
+    shape = blocks.shape
+    return blocks.reshape(*shape[:dim], shape[dim] * shape[dim + 1], *shape[dim + 2 :])
+
+
+def doubled(x, axis):
+    size, index = (lax.axis_size(axis), lax.axis_index(axis))
+    tiles, distance = (x[None], 1)
+    while distance < size:
+        other = lax.ppermute(tiles, axis, [(i, i ^ distance) for i in range(size)])
+        low = index & distance == 0
+        tiles = jnp.concatenate([jnp.where(low, tiles, other), jnp.where(low, other, tiles)])
+        distance *= 2
+    return tiles
 
 
 def with_halo(shard, sides, width):
@@ -114,7 +131,7 @@
             lax.dynamic_slice_in_dim(piece, begin, size, 0), basis
         ).astype(jnp.bfloat16)
 
-    piece = lax.all_gather(templates, "scan", axis=0, tiled=True)
+    piece = joined_along(doubled(templates, "scan"), 0)
     by_template = correlate_into(initial, pat_spec, piece.shape[0], raw_rows(piece), inverse)
     corr_map = by_template.T
     groups = orientation[:, 0]

time: 102 us -> 105 us (1.029)
  the two profiles are of different devices: /device:TPU:5 before, /device:TPU:10 now
where the time goes in v1:
time: 105 us; the launch traced here: 104 us
  local copies, waits for them, and re-layouts  38.4 us (37%)
  waiting for transfers between devices  25.8 us (25%)
  matrix products  19.8 us (19%)
  starting transfers between devices  10.4 us (10%)
  other arithmetic  8.82 us (8%)
    ppermute x4, waiting for transfers between devices, doubled(): other = lax.ppermute(tiles, axis, [(i, i ^ distance) for i in range(size)])  21.9 us
    dot_general x4, matrix products, mode_products(): jnp.einsum('kpr,ktr->ktp', left, right, preferred_element_type=jnp.float32)  10.6 us
    slice x2, local copies, waits for them, and re-layouts, correlate(): pat_sin = pat_spec[half + 1:]  8.51 us
    dot_general x2, matrix products, spectrum(): lax.dot_general(basis, flat, (((0,), (1,)), ((), ())), preferred_element_...  6.72 us
    concatenate x3, local copies, waits for them, and re-layouts, correlate(): cross = jnp.concatenate([real_part, imag_part], axis=0).astype(jnp.bfloat16)  5.75 us
    slice x1, local copies, waits for them, and re-layouts, correlate(): pat_cos = pat_spec[:half + 1]  4.96 us
    slice x2, local copies, waits for them, and re-layouts, correlate(): sin_cos = mode_products(pat_sin, tmpl_cos[1:half])  4.88 us
    ppermute x4, starting transfers between devices, doubled(): other = lax.ppermute(tiles, axis, [(i, i ^ distance) for i in range(size)])  4.76 us
  transfers between devices with their start and end apart: 6, of which 2 were waited for; matrix products, arithmetic and copies ran while one was open for 27% of the time, Pallas kernels for 0%

profile of v1, /device:TPU:10, one launch (start us, length us, event | category | flops | bytes accessed | tf_op | source)
XLA Modules:
  0.0 104.0 jit_solution(4095707619755338960)
XLA Ops:
  0.9 1.6 %cosine_convert_fusion = bf16[256,129]{1,0:T(8,128)(2,1)} fusion(), kind=kLoop, calls=%fused_computation.30 | loop fusion | flops 495360 | bytes 66048 | tf_op jit(solution)/shard_map/convert.6
  5.3 1.6 %collective-permute-start.1 = (bf16[2,2,64,256]{3,2,1,0:T(8,128)(2,1)S(1)}, bf16[2,2,64,256]{3,2,1,0:T(8,128)(2,1)}, u32[]{:S(2)}, u32[]{:S(2)}) collective-permute-start(bf16[2,2,64,256]{3,2,1,0:T(8,128)(2,1)S(1)} %pad_maximum_fusion.3), channel_id=1, source_target_pairs={{0,2},{1,3},{2,0},{3,1},{4,6},{5,7},{6,4},{7,5},{8,10},{9,11},{10,... | collective-permute-start | bytes 393224 | tf_op jit(solution)/shard_map/ppermute | solution.py:23
  6.9 6.2 %multiply_convert_fusion = bf16[256,96,64]{0,1,2:T(8,128)(2,1)} fusion(f32[64]{0:T(128)S(1)} %select_reduce_fusion.1, bf16[96,64,256]{2,1,0:T(8,128)(2,1)S(1)} %copy-done, bf16[256,127]{1,0:T(8,128)(2,1)} %fusion.31, bf16[256,129]{1,0:T(8,128)(2,1)} %cosine_convert_fusion), kind=kOutput, calls=%fused_computation | convolution fusion | flops 808714240 | bytes 6422784 | tf_op jit(solution)/shard_map/dot_general | solution.py:64
  15.2 4.5 %fusion.41 = (bf16[127,96,64]{0,1,2:T(8,128)(2,1)}, bf16[127,96,64]{0,1,2:T(8,128)(2,1)}) fusion(bf16[256,96,64]{0,1,2:T(8,128)(2,1)} %multiply_convert_fusion), kind=kLoop, calls=%fused_computation.71 | loop fusion | bytes 6242304 | tf_op jit(solution)/shard_map/while/body/eval_jaxpr/slice | solution.py:79
  19.7 4.0 %copy.33 = bf16[127,96,64]{1,2,0:T(8,128)(2,1)} copy(bf16[127,96,64]{0,1,2:T(8,128)(2,1)} %get-tuple-element.28) | data formatting | bytes 3121152 | tf_op jit(solution)/shard_map/while/body/eval_jaxpr/slice | solution.py:84
  23.7 4.0 %copy.31 = bf16[127,96,64]{1,2,0:T(8,128)(2,1)} copy(bf16[127,96,64]{0,1,2:T(8,128)(2,1)} %get-tuple-element.20) | data formatting | bytes 3121152 | tf_op jit(solution)/shard_map/while/body/eval_jaxpr/slice | solution.py:79
  27.7 5.0 %copy.29 = bf16[129,96,64]{1,2,0:T(8,128)(2,1)} copy(bf16[129,96,64]{0,1,2:T(8,128)(2,1)} %bitcast.23) | data formatting | bytes 3170304 | tf_op jit(solution)/shard_map/while/body/eval_jaxpr/slice | solution.py:78
  33.7 2.7 %collective-permute-start.3 = (bf16[8,2,64,256]{3,2,1,0:T(8,128)(2,1)S(1)}, bf16[8,2,64,256]{3,2,1,0:T(8,128)(2,1)S(1)}, u32[]{:S(2)}, u32[]{:S(2)}) collective-permute-start(bf16[8,2,64,256]{3,2,1,0:T(8,128)(2,1)S(1)} %pad_maximum_fusion.1), channel_id=1, source_target_pairs={{0,8},{1,9},{2,10},{3,11},{4,12},{5,13},{6,14},{7,15},{8,0},{9,1},... | collective-permute-start | bytes 1572872 | tf_op jit(solution)/shard_map/ppermute | solution.py:23
  37.0 21.9 %collective-permute-done.3 = bf16[8,2,64,256]{3,2,1,0:T(8,128)(2,1)S(1)} collective-permute-done((bf16[8,2,64,256]{3,2,1,0:T(8,128)(2,1)S(1)}, bf16[8,2,64,256]{3,2,1,0:T(8,128)(2,1)S(1)}, u32[]{:S(2)}, u32[]{:S(2)}) %collective-permute-start.3) | collective-permute-done | bytes 524320 | tf_op jit(solution)/shard_map/ppermute | solution.py:23
  60.6 1.4 %fusion.42 = (bf16[127,32,64]{0,2,1:T(8,128)(2,1)}, bf16[127,32,64]{0,2,1:T(8,128)(2,1)}) fusion(bf16[256,32,64]{0,2,1:T(8,128)(2,1)S(1)} %convolution_convert_fusion), kind=kLoop, calls=%fused_computation.72 | loop fusion | bytes 2080768 | tf_op jit(solution)/shard_map/while/body/eval_jaxpr/slice | solution.py:85
  62.0 3.5 %copy.30 = bf16[127,32,64]{2,1,0:T(8,128)(2,1)} copy(bf16[127,32,64]{0,2,1:T(8,128)(2,1)} %get-tuple-element.30) | data formatting | bytes 1040384 | tf_op jit(solution)/shard_map/while/body/eval_jaxpr/slice | solution.py:81
  65.5 3.5 %copy.34 = bf16[127,32,64]{2,1,0:T(8,128)(2,1)} copy(bf16[127,32,64]{0,2,1:T(8,128)(2,1)} %get-tuple-element.29) | data formatting | bytes 1040384 | tf_op jit(solution)/shard_map/while/body/eval_jaxpr/slice | solution.py:85
  69.0 2.7 %fusion.45 = f32[127,32,96]{2,1,0:T(8,128)S(1)} fusion(bf16[127,32,64]{2,1,0:T(8,128)(2,1)} %copy.30, bf16[127,96,64]{1,2,0:T(8,128)(2,1)} %copy.33), kind=kOutput, calls=%fused_computation.75 | convolution fusion | flops 49938432 | bytes 3641344 | tf_op jit(solution)/shard_map/while/body/eval_jaxpr/kpr,ktr->ktp/dot_general | solution.py:71
  71.7 2.0 %fusion.44 = f32[127,32,96]{2,1,0:T(8,128)} fusion(bf16[127,32,64]{2,1,0:T(8,128)(2,1)S(1)} %copy-done.3, bf16[127,96,64]{1,2,0:T(8,128)(2,1)S(1)} %copy-done.1), kind=kOutput, calls=%fused_computation.74 | convolution fusion | flops 49938432 | bytes 3641344 | tf_op jit(solution)/shard_map/while/body/eval_jaxpr/kpr,ktr->ktp/dot_general | solution.py:71
  73.8 1.6 %subtract_convert_fusion = bf16[127,32,96]{2,1,0:T(8,128)(2,1)} fusion(f32[127,32,96]{2,1,0:T(8,128)S(1)} %fusion.45, bf16[127,32,64]{2,1,0:T(8,128)(2,1)S(1)} %copy-done.4, bf16[127,96,64]{1,2,0:T(8,128)(2,1)S(1)} %copy-done.1), kind=kOutput, calls=%fused_computation.5 | convolution fusion | flops 50718720 | bytes 4421632 | tf_op jit(solution)/shard_map/while/body/eval_jaxpr/kpr,ktr->ktp/dot_general | solution.py:71
  75.4 2.7 %copy.36 = bf16[127,32,96]{0,2,1:T(8,128)(2,1)} copy(bf16[127,32,96]{2,1,0:T(8,128)(2,1)} %subtract_convert_fusion) | data formatting | bytes 1560576 | tf_op jit(solution)/shard_map/convert.4
  78.1 2.4 %copy.37 = bf16[127,3072]{1,0:T(8,128)(2,1)} copy(bf16[127,3072]{0,1:T(8,128)(2,1)} %bitcast.26) | data formatting | bytes 1560576 | tf_op jit(solution)/shard_map/while/body/eval_jaxpr/concatenate | solution.py:89
  80.5 2.9 %copy.28 = bf16[129,32,64]{2,1,0:T(8,128)(2,1)} copy(bf16[129,32,64]{0,2,1:T(8,128)(2,1)} %bitcast.24) | data formatting | bytes 1056768 | tf_op jit(solution)/shard_map/while/body/eval_jaxpr/slice | solution.py:80
  83.3 4.2 %fusion.4 = bf16[129,32,96]{2,1,0:T(8,128)(2,1)} fusion(f32[1,32,96]{2,1,0:T(8,128)S(1)} %broadcast.63, f32[127,32,96]{2,1,0:T(8,128)} %fusion.44, bf16[129,32,64]{2,1,0:T(8,128)(2,1)} %copy.28, bf16[129,96,64]{1,2,0:T(8,128)(2,1)} %copy.29), kind=kOutput, calls=%fused_computation.4 | convolution fusion | flops 52310016 | bytes 4478976 | tf_op jit(solution)/shard_map/while/body/eval_jaxpr/kpr,ktr->ktp/dot_general | solution.py:71
  87.6 3.4 %concatenate.49 = bf16[129,3072]{1,0:T(8,128)(2,1)} reshape(bf16[129,32,96]{2,1,0:T(8,128)(2,1)} %fusion.4) | data formatting | bytes 1585152 | tf_op jit(solution)/shard_map/while/body/eval_jaxpr/concatenate | solution.py:89
  91.0 2.5 %fusion.13 = f32[3072]{0:T(1024)S(1)} fusion(bf16[1,3072]{1,0:T(2,128)(2,1)S(1)} %concatenate.50, bf16[127,3072]{1,0:T(8,128)(2,1)} %copy.37, bf16[129,3072]{1,0:T(8,128)(2,1)} %concatenate.49, f32[129,256]{1,0:T(8,128)S(1)} %get-tuple-element.49, f32[129,256]{1,0:T(8,128)S(1)} %get-tuple-element.50), kind=kOutput, calls=%fused_computation.15 | convolution fusion | flops 413121024 | bytes 1855488 | tf_op jit(solution)/shard_map/while/body/eval_jaxpr/dot_general | solution.py:91
  93.7 3.7 %collective-permute-start.5 = (f32[1,16]{0,1:T(8,128)S(1)}, f32[1,16]{0,1:T(8,128)S(1)}, u32[]{:S(2)}, u32[]{:S(2)}) collective-permute-start(f32[1,16]{0,1:T(8,128)S(1)} %get-tuple-element.48), channel_id=1, source_target_pairs={{1,0},{2,1},{3,2},{4,3},{5,4},{6,5},{7,6},{8,7},{9,8},{10,9},{11,1... | collective-permute-start | bytes 200 | tf_op jit(solution)/shard_map/ppermute | solution.py:38
  97.5 1.9 %collective-permute-start.4 = (f32[1,16]{0,1:T(8,128)S(1)}, f32[1,16]{0,1:T(8,128)S(1)}, u32[]{:S(2)}, u32[]{:S(2)}) collective-permute-start(f32[1,16]{0,1:T(8,128)S(1)} %get-tuple-element.47), channel_id=1, source_target_pairs={{0,1},{1,2},{2,3},{3,4},{4,5},{5,6},{6,7},{7,8},{8,9},{9,10},{10,1... | collective-permute-start | bytes 200 | tf_op jit(solution)/shard_map/ppermute | solution.py:37
  99.4 3.9 %collective-permute-done.4 = f32[1,16]{0,1:T(8,128)S(1)} collective-permute-done((f32[1,16]{0,1:T(8,128)S(1)}, f32[1,16]{0,1:T(8,128)S(1)}, u32[]{:S(2)}, u32[]{:S(2)}) %collective-permute-start.4) | collective-permute-done | bytes 96 | tf_op jit(solution)/shard_map/ppermute | solution.py:37
  (46 shorter events, 9.4 us)
Async XLA Ops:
  0.6 6.3 %copy-start = (bf16[96,64,256]{2,1,0:T(8,128)(2,1)S(1)}, bf16[96,64,256]{2,1,0:T(8,128)(2,1)}, u32[]{:S(2)}) copy-start(bf16[96,64,256]{2,1,0:T(8,128)(2,1)} %param.5) | copy-start | bytes 9437188
  0.6 3.7 %collective-permute-start = (bf16[1,2,64,256]{3,2,1,0:T(8,128)(2,1)}, bf16[1,2,64,256]{3,2,1,0:T(8,128)(2,1)}, u32[]{:S(2)}, u32[]{:S(2)}) collective-permute-start(bf16[1,2,64,256]{3,2,1,0:T(8,128)(2,1)} %bitcast.30), channel_id=1, source_target_pairs={{0,1},{1,0},{2,3},{3,2},{4,5},{5,4},{6,7},{7,6},{8,9},{9,8},{10,11... | collective-permute-start | bytes 196616 | tf_op jit(solution)/shard_map/ppermute | solution.py:23
  5.3 7.8 %collective-permute-start.1 = (bf16[2,2,64,256]{3,2,1,0:T(8,128)(2,1)S(1)}, bf16[2,2,64,256]{3,2,1,0:T(8,128)(2,1)}, u32[]{:S(2)}, u32[]{:S(2)}) collective-permute-start(bf16[2,2,64,256]{3,2,1,0:T(8,128)(2,1)S(1)} %pad_maximum_fusion.3), channel_id=1, source_target_pairs={{0,2},{1,3},{2,0},{3,1},{4,6},{5,7},{6,4},{7,5},{8,10},{9,11},{10,... | collective-permute-start | bytes 393224 | tf_op jit(solution)/shard_map/ppermute | solution.py:23
  14.8 17.9 %collective-permute-start.2 = (bf16[4,2,64,256]{3,2,1,0:T(8,128)(2,1)}, bf16[4,2,64,256]{3,2,1,0:T(8,128)(2,1)}, u32[]{:S(2)}, u32[]{:S(2)}) collective-permute-start(bf16[4,2,64,256]{3,2,1,0:T(8,128)(2,1)} %pad_maximum_fusion.2), channel_id=1, source_target_pairs={{0,4},{1,5},{2,6},{3,7},{4,0},{5,1},{6,2},{7,3},{8,12},{9,13},{10,... | collective-permute-start | bytes 786440 | tf_op jit(solution)/shard_map/ppermute | solution.py:23
  32.7 3.7 %copy-start.8 = (s32[32,1]{0,1:T(1,128)S(1)}, s32[32,1]{0,1:T(1,128)}, u32[]{:S(2)}) copy-start(s32[32,1]{0,1:T(1,128)} %param.9) | copy-start | bytes 388
  33.7 25.2 %collective-permute-start.3 = (bf16[8,2,64,256]{3,2,1,0:T(8,128)(2,1)S(1)}, bf16[8,2,64,256]{3,2,1,0:T(8,128)(2,1)S(1)}, u32[]{:S(2)}, u32[]{:S(2)}) collective-permute-start(bf16[8,2,64,256]{3,2,1,0:T(8,128)(2,1)S(1)} %pad_maximum_fusion.1), channel_id=1, source_target_pairs={{0,8},{1,9},{2,10},{3,11},{4,12},{5,13},{6,14},{7,15},{8,0},{9,1},... | collective-permute-start | bytes 1572872 | tf_op jit(solution)/shard_map/ppermute | solution.py:23
  37.0 22.1 %copy-start.5 = (bf16[256,129]{1,0:T(8,128)(2,1)S(1)}, bf16[256,129]{1,0:T(8,128)(2,1)}, u32[]{:S(2)}) copy-start(bf16[256,129]{1,0:T(8,128)(2,1)} %cosine_convert_fusion) | copy-start | bytes 198148
  37.0 22.1 %copy-start.6 = (bf16[256,127]{1,0:T(8,128)(2,1)S(1)}, bf16[256,127]{1,0:T(8,128)(2,1)}, u32[]{:S(2)}) copy-start(bf16[256,127]{1,0:T(8,128)(2,1)} %fusion.31) | copy-start | bytes 195076
  59.6 1.0 copy-start.2
  69.0 2.7 %copy-start.1 = (bf16[127,96,64]{1,2,0:T(8,128)(2,1)S(1)}, bf16[127,96,64]{1,2,0:T(8,128)(2,1)}, u32[]{:S(2)}) copy-start(bf16[127,96,64]{1,2,0:T(8,128)(2,1)} %copy.31) | copy-start | bytes 4681732
  69.0 2.8 %copy-start.3 = (bf16[127,32,64]{2,1,0:T(8,128)(2,1)S(1)}, bf16[127,32,64]{2,1,0:T(8,128)(2,1)}, u32[]{:S(2)}) copy-start(bf16[127,32,64]{2,1,0:T(8,128)(2,1)} %copy.30) | copy-start | bytes 1560580
  71.7 2.0 %copy-start.4 = (bf16[127,32,64]{2,1,0:T(8,128)(2,1)S(1)}, bf16[127,32,64]{2,1,0:T(8,128)(2,1)}, u32[]{:S(2)}) copy-start(bf16[127,32,64]{2,1,0:T(8,128)(2,1)} %copy.34) | copy-start | bytes 1560580
  93.5 10.5 %copy-start.7 = (f32[32,96]{1,0:T(8,128)}, f32[32,96]{1,0:T(8,128)S(1)}, u32[]{:S(2)}) copy-start(f32[32,96]{1,0:T(8,128)S(1)} %reshape.53) | copy-start | bytes 36868
  93.7 5.7 %collective-permute-start.5 = (f32[1,16]{0,1:T(8,128)S(1)}, f32[1,16]{0,1:T(8,128)S(1)}, u32[]{:S(2)}, u32[]{:S(2)}) collective-permute-start(f32[1,16]{0,1:T(8,128)S(1)} %get-tuple-element.48), channel_id=1, source_target_pairs={{1,0},{2,1},{3,2},{4,3},{5,4},{6,5},{7,6},{8,7},{9,8},{10,9},{11,1... | collective-permute-start | bytes 200 | tf_op jit(solution)/shard_map/ppermute | solution.py:38
  97.5 5.9 %collective-permute-start.4 = (f32[1,16]{0,1:T(8,128)S(1)}, f32[1,16]{0,1:T(8,128)S(1)}, u32[]{:S(2)}, u32[]{:S(2)}) collective-permute-start(f32[1,16]{0,1:T(8,128)S(1)} %get-tuple-element.47), channel_id=1, source_target_pairs={{0,1},{1,2},{2,3},{3,4},{4,5},{5,6},{6,7},{7,8},{8,9},{9,10},{10,1... | collective-permute-start | bytes 200 | tf_op jit(solution)/shard_map/ppermute | solution.py:37
